TPU v7x, 32 devices: a whole 2x2x4 slice. The times are simulated.
32 devices in a mesh: dp: 8 (over z, x), mp: 4 (over y, core).
Axes of the slice: x: 2, y: 2, z: 4, core: 2. Of those that a mesh axis runs over, the one named last changes fastest.
Arguments:
- latent: bfloat16 [65536, 512], P('dp'), may hold values from -6 to 6
- actions: bfloat16 [6, 65536], P(None, 'dp'), may hold values from -1 to 1
- task_ids: int32 [65536], P('dp'), may hold values from 0 to 79
- action_masks: int32 [80, 6], replicated, may hold values 0 or 1
- next_latent: bfloat16 [65536, 512], P('dp', 'mp'), may hold values from 0 to 0.25
- reward_bins: int32 [65536], P('dp'), may hold values from 0 to 99
- reward_frac: float32 [65536], P('dp'), may hold values from 0 to 1
- task_embed: bfloat16 [80, 96], replicated, may hold values from -6 to 6
- dyn_w1: bfloat16 [614, 1024], P(None, 'mp'), may hold values from -0.25 to 0.25
- dyn_b1: float32 [1024], P('mp'), may hold values from -3 to 3
- dyn_gain: float32 [1024], P('mp'), may hold values from 0.5 to 1.5
- dyn_shift: float32 [1024], P('mp'), may hold values from -2 to 2
- rew_w1: bfloat16 [614, 1024], P(None, 'mp'), may hold values from -0.25 to 0.25
- rew_b1: float32 [1024], P('mp'), may hold values from -3 to 3
- rew_gain: float32 [1024], P('mp'), may hold values from 0.5 to 1.5
- rew_shift: float32 [1024], P('mp'), may hold values from -2 to 2
- dyn_w2: bfloat16 [1024, 512], P('mp'), may hold values from -0.375 to 0.375
- dyn_b2: float32 [512], replicated, may hold values from -2 to 2
- rew_w2: bfloat16 [1024, 101], P('mp'), may hold values from -0.375 to 0.375
- rew_b2: float32 [101], replicated, may hold values from -2 to 2
Outputs:
- latents: bfloat16 [65536, 512], P('dp', 'mp')
- latent_grad: bfloat16 [65536, 512], P('dp', 'mp')
- losses: float32 [2], replicated
- grad_task_embed: float32 [80, 96], replicated
- grad_dyn_w1: float32 [614, 1024], P(None, 'mp')
- grad_dyn_b1: float32 [1024], P('mp')
- grad_dyn_gain: float32 [1024], P('mp')
- grad_dyn_shift: float32 [1024], P('mp')
- grad_rew_w1: float32 [614, 1024], P(None, 'mp')
- grad_rew_b1: float32 [1024], P('mp')
- grad_rew_gain: float32 [1024], P('mp')
- grad_rew_shift: float32 [1024], P('mp')
- grad_dyn_w2: float32 [1024, 512], P('mp')
- grad_dyn_b2: float32 [512], replicated
- grad_rew_w2: float32 [1024, 101], P('mp')
- grad_rew_b2: float32 [101], replicated
Inputs may be any that keep to these rules, and one draw needn't show every extreme that they name: The upper bin reward_bins + 1 is a valid bin.
All inputs are finite; a program needn't handle non-finite values.
Results may differ from a plain program's by a relative error of at most 0.024.
Values may be sent and summed in bfloat16 or wider, within the bound.
A program may use at most 192 MiB of HBM per device.

v0:
```python
import jax
import jax.numpy as jnp
from jax import lax
from jax.sharding import PartitionSpec as P

HID = 1024
GROUP = 8
CONS_COEF = 20.0
REW_COEF = 0.1


def mish_act(values):
    return values * jnp.tanh(jax.nn.softplus(values))


def contract(left, right, left_dim, right_dim):
    return lax.dot_general(
        left, right, (((left_dim,), (right_dim,)), ((), ())), preferred_element_type=jnp.float32
    )


def on_device(
    latent,
    actions,
    task_ids,
    action_masks,
    next_latent,
    reward_bins,
    reward_frac,
    task_embed,
    dyn_w1,
    dyn_b1,
    dyn_gain,
    dyn_shift,
    rew_w1,
    rew_b1,
    rew_gain,
    rew_shift,
    dyn_w2,
    dyn_b2,
    rew_w2,
    rew_b2,
):
    tok_rows = latent.shape[0]
    shard_width = dyn_w1.shape[1]
    share_width = next_latent.shape[1]
    n_model = lax.axis_size("mp")
    total_rows = tok_rows * lax.axis_size("dp")
    mp_index = lax.axis_index("mp")
    lat_width = latent.shape[1]
    act_width = actions.shape[0]
    onehot = (
        task_ids[:, None] == jnp.arange(task_embed.shape[0], dtype=jnp.int32)[None, :]
    ).astype(jnp.bfloat16)
    embedded = jnp.dot(onehot, task_embed, preferred_element_type=jnp.float32).astype(jnp.bfloat16)
    mask_cols = contract(action_masks.astype(jnp.bfloat16), onehot, 0, 1)
    masked = (actions.astype(jnp.float32) * mask_cols).astype(jnp.bfloat16)
    w_first = jnp.concatenate([dyn_w1, rew_w1], axis=1)
    w_lat = w_first[:lat_width]
    w_act = w_first[lat_width : lat_width + act_width]
    w_task = w_first[lat_width + act_width :]
    bias_pair = jnp.concatenate([dyn_b1, rew_b1])
    pre_act = (
        jnp.dot(latent, w_lat, preferred_element_type=jnp.float32)
        + contract(masked, w_act, 0, 0)
        + jnp.dot(embedded, w_task, preferred_element_type=jnp.float32)
        + bias_pair
    )
    pre_act = pre_act.reshape(tok_rows, 2, shard_width)
    first_sum, second_sum = lax.psum(
        (jnp.sum(pre_act, axis=2).T, jnp.sum(pre_act * pre_act, axis=2).T), "mp"
    )
    average = first_sum / HID
    variance = second_sum / HID - average * average
    inv_std = lax.rsqrt(variance + 1e-05).T[:, :, None]
    normalized = (pre_act - average.T[:, :, None]) * inv_std
    gain_pair = jnp.stack([dyn_gain, rew_gain])
    shift_pair = jnp.stack([dyn_shift, rew_shift])
    normed = normalized * gain_pair + shift_pair
    hidden = mish_act(normed).astype(jnp.bfloat16)
    hidden_dyn = hidden[:, 0]
    hidden_rew = hidden[:, 1]
    lat_part = jnp.dot(hidden_dyn, dyn_w2, preferred_element_type=jnp.float32).astype(jnp.bfloat16)
    lat_share = lax.psum_scatter(lat_part, "mp", scatter_dimension=1, tiled=True).astype(
        jnp.float32
    )
    lat_share = lat_share + lax.dynamic_slice_in_dim(dyn_b2, mp_index * share_width, share_width)
    logit_part = jnp.dot(hidden_rew, rew_w2, preferred_element_type=jnp.float32)
    logits = lax.psum(logit_part, "mp") + rew_b2
    groups = lat_share.reshape(tok_rows, share_width // GROUP, GROUP)
    simplex = jax.nn.softmax(groups, axis=-1)
    latents_out = simplex.reshape(tok_rows, share_width)
    lat_error = latents_out - next_latent.astype(jnp.float32)
    cons_part = jnp.sum(lat_error * lat_error)
    log_probs = jax.nn.log_softmax(logits, axis=-1)
    bin_iota = jnp.arange(logits.shape[1], dtype=jnp.int32)[None, :]
    target = jnp.where(bin_iota == reward_bins[:, None], 1.0 - reward_frac[:, None], 0.0)
    target = target + jnp.where(bin_iota == reward_bins[:, None] + 1, reward_frac[:, None], 0.0)
    rew_part = -jnp.sum(target * log_probs) / n_model
    d_groups = (2.0 * CONS_COEF / total_rows * lat_error).reshape(groups.shape)
    d_lat = simplex * (d_groups - jnp.sum(simplex * d_groups, axis=-1, keepdims=True))
    d_share = d_lat.reshape(tok_rows, share_width).astype(jnp.bfloat16)
    d_full = lax.all_gather(d_share, "mp", axis=1, tiled=True)
    d_logits = (REW_COEF / total_rows * (jnp.exp(log_probs) - target)).astype(jnp.bfloat16)
    grad_w2_dyn = contract(hidden_dyn, d_full, 0, 0)
    grad_b2_dyn = jnp.sum(d_full.astype(jnp.float32), axis=0)
    grad_w2_rew = contract(hidden_rew, d_logits, 0, 0)
    grad_b2_rew = jnp.sum(d_logits.astype(jnp.float32), axis=0)
    head_grads = (grad_w2_dyn, grad_b2_dyn, grad_w2_rew, grad_b2_rew)
    d_hid_dyn = contract(d_full, dyn_w2, 1, 1)
    d_hid_rew = contract(d_logits, rew_w2, 1, 1)
    d_hidden = jnp.stack([d_hid_dyn, d_hid_rew], axis=1)
    unused_value, mish_back = jax.vjp(mish_act, normed)
    d_normed = mish_back(d_hidden)[0]
    grad_gain = jnp.sum(d_normed * normalized, axis=0)
    grad_shift = jnp.sum(d_normed, axis=0)
    d_unit = d_normed * gain_pair
    back_first, back_second = lax.psum(
        (jnp.sum(d_unit, axis=2).T, jnp.sum(d_unit * normalized, axis=2).T), "mp"
    )
    d_pre = inv_std * (
        d_unit - (back_first.T / HID)[:, :, None] - normalized * (back_second.T / HID)[:, :, None]
    )
    d_pre = d_pre.reshape(tok_rows, 2 * shard_width).astype(jnp.bfloat16)
    grad_b1 = jnp.sum(d_pre.astype(jnp.float32), axis=0)
    grad_w_lat = contract(latent, d_pre, 0, 0)
    grad_w_act = jnp.dot(masked, d_pre, preferred_element_type=jnp.float32)
    task_sums = contract(onehot, d_pre, 0, 0)
    grad_w_task = jnp.dot(
        task_embed.astype(jnp.float32).T, task_sums, precision=lax.Precision.HIGHEST
    )
    embed_part = jnp.dot(task_sums, w_task.astype(jnp.float32).T, precision=lax.Precision.HIGHEST)
    grad_w1 = jnp.concatenate([grad_w_lat, grad_w_act, grad_w_task], axis=0)
    input_part = contract(d_pre, w_lat, 1, 1).astype(jnp.bfloat16)
    input_share = lax.psum_scatter(input_part, "mp", scatter_dimension=1, tiled=True).astype(
        jnp.float32
    )
    latent_grad = (input_share * total_rows).astype(jnp.bfloat16)
    cons_sum, rew_sum, grad_embed = lax.psum((cons_part, rew_part, embed_part), ("dp", "mp"))
    losses = jnp.stack([cons_sum, rew_sum]) / total_rows
    summed = lax.psum(
        (
            grad_w1,
            grad_b1,
            grad_gain,
            grad_shift,
            head_grads[0],
            head_grads[1],
            head_grads[2],
            head_grads[3],
        ),
        "dp",
    )
    grad_w1, grad_b1, grad_gain, grad_shift = (summed[0], summed[1], summed[2], summed[3])
    head_grads = (summed[4], summed[5], summed[6], summed[7])
    return (
        latents_out.astype(jnp.bfloat16),
        latent_grad,
        losses,
        grad_embed,
        grad_w1[:, :shard_width],
        grad_b1[:shard_width],
        grad_gain[0],
        grad_shift[0],
        grad_w1[:, shard_width:],
        grad_b1[shard_width:],
        grad_gain[1],
        grad_shift[1],
        head_grads[0],
        head_grads[1],
        head_grads[2],
        head_grads[3],
    )


def solution(mesh):
    return jax.shard_map(
        on_device,
        mesh=mesh,
        in_specs=(
            P("dp", None),
            P(None, "dp"),
            P("dp"),
            P(),
            P("dp", "mp"),
            P("dp"),
            P("dp"),
            P(),
            P(None, "mp"),
            P("mp"),
            P("mp"),
            P("mp"),
            P(None, "mp"),
            P("mp"),
            P("mp"),
            P("mp"),
            P("mp", None),
            P(),
            P("mp", None),
            P(),
        ),
        out_specs=(
            P("dp", "mp"),
            P("dp", "mp"),
            P(),
            P(),
            P(None, "mp"),
            P("mp"),
            P("mp"),
            P("mp"),
            P(None, "mp"),
            P("mp"),
            P("mp"),
            P("mp"),
            P("mp", None),
            P(),
            P("mp", None),
            P(),
        ),
        check_vma=False,
    )
```

profile of v0, /device:TPU:0, one launch (start us, length us, event | category | flops | bytes accessed | tf_op | source)
XLA Modules:
  0.0 630.1 jit_solution(13819635788461500749)
XLA Ops:
  7.2 1.0 constant_dynamic-update-slice_fusion.1
  8.3 0.7 pad_maximum_fusion.2
  9.0 1.0 constant_dynamic-update-slice_fusion
  10.0 11.8 %fusion.39 = f32[512,8192]{1,0:T(8,128)} fusion(bf16[8192,512]{1,0:T(8,128)(2,1)} %param.20, bf16[614,512]{1,0:T(8,128)(2,1)S(1)} %constant_dynamic-update-slice_fusion), kind=kOutput, calls=%fused_computation.95 | convolution fusion | flops 4294967296 | bytes 25690112 | tf_op jit(solution)/shard_map/dot_general | solution.py:64
  21.8 7.3 %fusion.33 = f32[8192,512]{0,1:T(8,128)} fusion(bf16[80,96]{1,0:T(8,128)(2,1)S(1)} %copy-done.21, s32[8192]{0:T(1024)S(1)} %copy-done.16, bf16[614,512]{1,0:T(8,128)(2,1)S(1)} %constant_dynamic-update-slice_fusion), kind=kOutput, calls=%fused_computation.87 | convolution fusion | flops 932577280 | bytes 16928768 | tf_op jit(solution)/shard_map/dot_general | solution.py:66
  29.1 0.5 fusion.23
  29.7 19.8 %bitcast_reduce_fusion = (f32[8192,2]{0,1:T(2,128)}, f32[8192,2]{0,1:T(2,128)}, f32[8192,512]{0,1:T(8,128)}) fusion(f32[512]{0:T(512)S(1)} %pad_maximum_fusion.2, f32[8192,512]{0,1:T(8,128)} %fusion.33, bf16[6,8192]{1,0:T(8,128)(2,1)S(1)} %fusion.23, bf16[614,512]{1,0:T(8,128)(2,1)S(1)} %constant_dynamic-update-slice_fusion, f32[512,8192]{1,0:T(8,128)} %fusion.39), kind=kOutput, calls=%fused_computation.29 | convolution fusion | flops 75464704 | bytes 50604032 | tf_op jit(solution)/shard_map/dot_general | solution.py:17
  49.9 34.0 %all-reduce.16.cloned.1.call-done = (f32[2,8192]{1,0:T(2,128)}, f32[2,8192]{1,0:T(2,128)}) async-done(((f32[2,8192]{1,0:T(2,128)}, f32[2,8192]{1,0:T(2,128)}), (f32[2,8192]{1,0:T(2,128)}, f32[2,8192]{1,0:T(2,128)})) %all-reduce.16.cloned.1.call-update) | async-done | bytes 131088 | tf_op jit(solution)/shard_map/psum | solution.py:70
  83.9 0.9 multiply_bitcast_fusion.2
  84.9 14.7 %fusion.17 = bf16[8192,2,256]{0,2,1:T(8,128)(2,1)S(1)} fusion(f32[8192,512]{0,1:T(8,128)} %get-tuple-element.93, f32[2,256]{1,0:T(2,128)S(1)} %get-tuple-element.92, f32[2,256]{1,0:T(2,128)S(1)} %get-tuple-element.94, f32[8192,2]{0,1:T(2,128)S(1)} %get-tuple-element.82, f32[8192,2]{0,1:T(2,128)S(1)} %get-tuple-element.81), kind=kLoop, calls=%fused_computation.41 | loop fusion | flops 50331648 | bytes 25300992 | tf_op jit(solution)/shard_map/convert_element_type | solution.py:80
  99.6 3.2 copy-done.4
  102.8 5.6 convolution_convert_fusion.1
  108.4 12.1 %copy.47 = bf16[8192,512]{0,1:T(8,128)(2,1)} copy(bf16[8192,512]{1,0:T(8,128)(2,1)} %convolution_convert_fusion.1) | data formatting | bytes 16777216
  120.6 2.9 copy.45
  123.5 0.8 dynamic_slice.3
  124.3 5.6 fusion.29
  129.9 0.3 all-gather.2.cloned.1.call-start
  130.2 62.2 %reduce-scatter.7.cloned.1.call-done = bf16[128,8192]{1,0:T(8,128)(2,1)} async-done(((bf16[512,8192]{1,0:T(8,128)(2,1)}), bf16[128,8192]{1,0:T(8,128)(2,1)}) %reduce-scatter.7.cloned.1.call-update) | async-done | bytes 2097168
  192.4 3.0 bitcast_reduce_fusion.1
  195.4 3.4 fusion.26
  198.8 7.2 %fusion.21 = bf16[8192,128]{0,1:T(8,128)(2,1)} fusion(bf16[8192,128]{0,1:T(8,128)(2,1)S(1)} %copy.45, bf16[128,8192]{1,0:T(8,128)(2,1)} %reduce-scatter.7.cloned.1.call-done, f32[8192,16]{0,1:T(8,128)S(1)} %fusion.26, f32[8192,16]{0,1:T(8,128)S(1)} %bitcast_reduce_fusion.1, f32[128]{0:T(128)} %copy-done.24), kind=kOutput, calls=%fused_computation.52 | output fusion | flops 21102600 | bytes 7340544 | tf_op jit(solution)/shard_map/sub | solution.py:101
  206.0 0.5 all-reduce.14.cloned.1.call-start
  206.5 0.8 broadcast_add_fusion
  207.3 0.8 broadcast_subtract_fusion
  208.0 59.5 %all-reduce.10.cloned.1.call-done = f32[8192,101]{0,1:T(8,128)} async-done(((f32[8192,101]{0,1:T(8,128)}), f32[8192,101]{0,1:T(8,128)}) %all-reduce.10.cloned.1.call-update) | async-done | bytes 3309584 | tf_op jit(solution)/shard_map/psum | solution.py:89
  267.5 2.5 add_reduce_fusion
  270.0 2.6 exponential_reduce_fusion
  272.7 4.0 convert_reduce_fusion.2
  276.7 5.9 convolution_bitcast_fusion.1
  282.7 2.1 fusion.28
  284.7 43.2 %all-gather.2.cloned.1.call-done = bf16[8192,512]{0,1:T(8,128)(2,1)} async-done(((bf16[8192,128]{0,1:T(8,128)(2,1)}), bf16[8192,512]{0,1:T(8,128)(2,1)}) %all-gather.2.cloned.1.call-update) | async-done | bytes 8388624 | tf_op jit(solution)/shard_map/all_gather | solution.py:103
  328.0 9.2 %convolution_bitcast_fusion = f32[8192,1,256]{0,2,1:T(8,128)} fusion(bf16[256,512]{1,0:T(8,128)(2,1)S(1)} %copy-done, bf16[8192,512]{0,1:T(8,128)(2,1)} %all-gather.2.cloned.1.call-done), kind=kOutput, calls=%fused_computation.47 | convolution fusion | flops 2147483648 | bytes 17039360 | tf_op jit(solution)/shard_map/dot_general | solution.py:17
  337.2 29.3 %pad_maximum_fusion = (f32[8192,2,256]{0,2,1:T(8,128)}, f32[8192,2,256]{0,2,1:T(8,128)}) fusion(f32[8192,1,256]{0,2,1:T(8,128)} %convolution_bitcast_fusion.1, f32[8192,1,256]{0,2,1:T(8,128)} %convolution_bitcast_fusion, f32[2,256]{1,0:T(2,128)S(1)} %get-tuple-element.92, f32[2,256]{1,0:T(2,128)S(1)} %get-tuple-element.94, ...), kind=kLoop, calls=%fused_computation.19 | loop fusion | flops 104857600 | bytes 67244032 | tf_op jit(solution)/shard_map/stack | solution.py:112
  366.5 8.7 %fusion.51 = (f32[8192,2]{0,1:T(2,128)}, f32[8192,2]{0,1:T(2,128)}) fusion(f32[8192,2,256]{0,2,1:T(8,128)} %get-tuple-element.75, f32[8192,2]{0,1:T(2,128)S(1)} %get-tuple-element.82, f32[8192,2]{0,1:T(2,128)S(1)} %get-tuple-element.81, f32[8192,512]{0,1:T(8,128)S(1)} %bitcast.218), kind=kLoop, calls=%fused_computation.119 | loop fusion | flops 20938752 | bytes 33816576 | tf_op jit(solution)/shard_map/reduce_sum | solution.py:119
  375.3 7.8 %fusion.27 = f32[256,512]{1,0:T(8,128)} fusion(bf16[8192,512]{0,1:T(8,128)(2,1)} %all-gather.2.cloned.1.call-done, bf16[8192,2,256]{0,2,1:T(8,128)(2,1)} %copy-done.4), kind=kOutput, calls=%fused_computation.71 | convolution fusion | flops 2147483648 | bytes 13107200 | tf_op jit(solution)/shard_map/dot_general | solution.py:17
  383.1 28.7 %fusion.50 = (f32[512]{0:T(512)S(1)}, f32[512]{0:T(512)S(1)}, f32[8192,512]{0,1:T(8,128)}) fusion(f32[8192,2]{0,1:T(2,128)S(1)} %get-tuple-element.82, f32[8192,512]{0,1:T(8,128)} %get-tuple-element.93, f32[8192,2]{0,1:T(2,128)S(1)} %get-tuple-element.81, f32[512]{0:T(512)S(1)} %bitcast.230, f32[512]{0:T(512)S(1)} %bitcast.228, ...), kind=kLoop, calls=%fused_computation.118 | loop fusion | flops 109050880 | bytes 50470912 | tf_op jit(solution)/shard_map/reduce_sum | solution.py:116
  411.8 0.9 multiply_bitcast_fusion
  412.7 0.9 multiply_bitcast_fusion.1
  413.5 12.9 %convert_reduce_fusion.1 = (f32[512]{0:T(512)S(1)}, bf16[8192,512]{0,1:T(8,128)(2,1)S(1)}) fusion(f32[8192,2]{0,1:T(2,128)S(1)} %multiply_bitcast_fusion, f32[8192,512]{0,1:T(8,128)} %get-tuple-element.93, f32[8192,2]{0,1:T(2,128)S(1)} %get-tuple-element.81, f32[8192,2]{0,1:T(2,128)S(1)} %multiply_bitcast_fusion.1, f32[8192,512]{0,1:T(8,128)} %get-tuple-element.71, ...), kind=kLoop, calls=%fused_computation.37 | loop fusion | flops 41942528 | bytes 42209280 | tf_op jit(solution)/shard_map/reduce_sum | solution.py:125
  426.5 2.3 fusion.58
  428.7 0.9 copy-done.2
  429.7 2.7 fusion.30
  432.4 9.7 %convolution_bitcast_fusion.3 = f32[512,512]{1,0:T(8,128)S(1)} fusion(bf16[8192,512]{0,1:T(8,128)(2,1)} %copy-done.2, bf16[8192,512]{1,0:T(8,128)(2,1)} %param.20), kind=kOutput, calls=%fused_computation.88 | convolution fusion | flops 4294967296 | bytes 17825792 | tf_op jit(solution)/shard_map/dot_general | solution.py:17
  442.1 0.3 convolution_bitcast_fusion.4
  442.4 1.2 pad_maximum_fusion.1
  443.7 10.3 %convolution_convert_fusion = bf16[8192,512]{1,0:T(8,128)(2,1)} fusion(bf16[8192,512]{0,1:T(8,128)(2,1)} %copy-done.2, bf16[614,512]{1,0:T(8,128)(2,1)S(1)} %copy-done.8), kind=kOutput, calls=%fused_computation.45 | convolution fusion | flops 4299161600 | bytes 17301504 | tf_op jit(solution)/shard_map/dot_general | solution.py:17
  453.9 11.8 %copy.49 = bf16[8192,512]{0,1:T(8,128)(2,1)} copy(bf16[8192,512]{1,0:T(8,128)(2,1)} %convolution_convert_fusion) | data formatting | bytes 16777216
  466.6 0.8 copy-done.5
  467.4 4.5 multiply_reduce_fusion.2
  471.9 4.1 copy.46
  476.0 4.8 convert_reduce_fusion
  480.8 1.1 fusion.41
  481.9 41.2 %all-reduce = (f32[1]{0:T(128)}, f32[1]{0:T(128)}, f32[80,96]{1,0:T(8,128)}) all-reduce(f32[1]{0:T(128)} %bitcast.30, f32[1]{0:T(128)} %bitcast.29, f32[80,96]{1,0:T(8,128)S(1)} %fusion.41), channel_id=1, replica_groups=mesh['dp'=8,'mp'=4] {'dp','mp'}, use_global_device_ids=true, to_apply=%region_19.20 | all-reduce | flops 7682 | bytes 61456 | tf_op jit(solution)/shard_map/psum | solution.py:139
  523.1 22.9 %all-reduce.1 = (f32[512]{0:T(512)S(1)}, f32[2,256]{1,0:T(2,128)S(1)}, f32[2,256]{1,0:T(2,128)S(1)}, f32[512]{0:T(512)}, f32[101]{0:T(128)}) all-reduce(f32[512]{0:T(512)S(1)} %get-tuple-element.72, f32[2,256]{1,0:T(2,128)S(1)} %reduce_sum.142, f32[2,256]{1,0:T(2,128)S(1)} %reduce_sum.144, ...), channel_id=1, replica_groups=mesh['dp'=8,'mp'=4] {'dp'}, use_global_device_ids=true, to_apply=%region_23.24 | all-reduce | flops 2149 | bytes 17192 | tf_op jit(solution)/shard_map/psum | solution.py:141
  546.1 1.9 maximum_multiply_fusion
  548.0 0.6 fusion.57
  548.5 0.6 fusion.56
  549.1 0.6 fusion.55
  549.7 2.6 fusion.54
  552.2 64.2 %reduce-scatter.9.cloned.1.call-done = bf16[128,8192]{1,0:T(8,128)(2,1)} async-done(((bf16[512,8192]{1,0:T(8,128)(2,1)}), bf16[128,8192]{1,0:T(8,128)(2,1)}) %reduce-scatter.9.cloned.1.call-update) | async-done | bytes 2097168
  616.4 3.2 copy.50
  619.6 1.7 multiply_convert_fusion
  621.4 0.8 copy.62
  622.2 0.6 copy.63
  (95 shorter events, 0.8 us)
Async XLA Ops:
  7.2 95.6 %copy-start = (bf16[256,512]{1,0:T(8,128)(2,1)S(1)}, bf16[256,512]{1,0:T(8,128)(2,1)}, u32[]{:S(2)}) copy-start(bf16[256,512]{1,0:T(8,128)(2,1)} %param.36) | copy-start | bytes 786436
  7.2 76.7 %all-reduce.16.cloned.1.call-start = ((), (), s32[]{:S(2)}) async-start(), calls=%async_computation.8 | async-start | bytes 262144 | tf_op jit(solution)/shard_map/psum | solution.py:70
  10.0 19.7 %copy-start.7 = (bf16[614,512]{1,0:T(8,128)(2,1)}, bf16[614,512]{1,0:T(8,128)(2,1)S(1)}, u32[]{:S(2)}) copy-start(bf16[614,512]{1,0:T(8,128)(2,1)S(1)} %constant_dynamic-update-slice_fusion) | copy-start | bytes 1886212
  10.0 11.8 %copy-start.16 = (s32[8192]{0:T(1024)S(1)}, s32[8192]{0:T(1024)}, u32[]{:S(2)}) copy-start(s32[8192]{0:T(1024)} %param.22) | copy-start | bytes 98308
  10.0 11.8 %copy-start.21 = (bf16[80,96]{1,0:T(8,128)(2,1)S(1)}, bf16[80,96]{1,0:T(8,128)(2,1)}, u32[]{:S(2)}) copy-start(bf16[80,96]{1,0:T(8,128)(2,1)} %param.27) | copy-start | bytes 46084
  21.8 7.3 %copy-start.30 = (bf16[6,8192]{1,0:T(8,128)(2,1)S(1)}, bf16[6,8192]{1,0:T(8,128)(2,1)}, u32[]{:S(2)}) copy-start(bf16[6,8192]{1,0:T(8,128)(2,1)} %param.21) | copy-start | bytes 294916
  21.8 7.3 %copy-start.31 = (s32[80,6]{0,1:T(8,128)S(1)}, s32[80,6]{0,1:T(8,128)}, u32[]{:S(2)}) copy-start(s32[80,6]{0,1:T(8,128)} %param.23) | copy-start | bytes 5764
  29.6 19.9 %copy-start.11 = (bf16[6,8192]{1,0:T(8,128)(2,1)}, bf16[6,8192]{1,0:T(8,128)(2,1)S(1)}, u32[]{:S(2)}) copy-start(bf16[6,8192]{1,0:T(8,128)(2,1)S(1)} %fusion.23) | copy-start | bytes 294916
  29.6 20.2 %copy-start.26 = (f32[256]{0:T(256)S(1)}, f32[256]{0:T(256)}, u32[]{:S(2)}) copy-start(f32[256]{0:T(256)} %param.35) | copy-start | bytes 3076
  29.6 20.2 %copy-start.27 = (f32[256]{0:T(256)S(1)}, f32[256]{0:T(256)}, u32[]{:S(2)}) copy-start(f32[256]{0:T(256)} %param.31) | copy-start | bytes 3076
  29.7 20.2 %copy-start.28 = (f32[256]{0:T(256)S(1)}, f32[256]{0:T(256)}, u32[]{:S(2)}) copy-start(f32[256]{0:T(256)} %param.34) | copy-start | bytes 3076
  29.7 20.2 %copy-start.29 = (f32[256]{0:T(256)S(1)}, f32[256]{0:T(256)}, u32[]{:S(2)}) copy-start(f32[256]{0:T(256)} %param.30) | copy-start | bytes 3076
  49.6 142.8 %reduce-scatter.7.cloned.1.call-start = ((), (), s32[]{:S(2)}) async-start(), calls=%async_computation.4 | async-start | bytes 10485760
  99.6 3.2 copy-start.4
  120.5 3.8 copy-start.14
  120.5 147.0 %all-reduce.10.cloned.1.call-start = ((), (), s32[]{:S(2)}) async-start(), calls=%async_computation.3 | async-start | bytes 6815744 | tf_op jit(solution)/shard_map/psum | solution.py:89
  123.5 75.3 %copy-start.6 = (bf16[8192,128]{0,1:T(8,128)(2,1)}, bf16[8192,128]{0,1:T(8,128)(2,1)S(1)}, u32[]{:S(2)}) copy-start(bf16[8192,128]{0,1:T(8,128)(2,1)S(1)} %copy.45) | copy-start | bytes 6291460
  124.3 68.1 %copy-start.24 = (f32[128]{0:T(128)}, f32[128]{0:T(128)S(1)}, u32[]{:S(2)}) copy-start(f32[128]{0:T(128)S(1)} %dynamic_slice.3) | copy-start | bytes 1540
  129.9 198.0 %all-gather.2.cloned.1.call-start = ((), (), s32[]{:S(2)}) async-start(), calls=%async_computation.2 | async-start | bytes 10485760 | tf_op jit(solution)/shard_map/all_gather | solution.py:103
  205.9 66.8 %copy-start.18 = (f32[8192]{0:T(1024)S(1)}, f32[8192]{0:T(1024)}, u32[]{:S(2)}) copy-start(f32[8192]{0:T(1024)} %param.26) | copy-start | bytes 98308
  205.9 66.8 %copy-start.19 = (s32[8192]{0:T(1024)S(1)}, s32[8192]{0:T(1024)}, u32[]{:S(2)}) copy-start(s32[8192]{0:T(1024)} %param.25) | copy-start | bytes 98308
  205.9 66.8 %copy-start.23 = (f32[101]{0:T(128)S(1)}, f32[101]{0:T(128)}, u32[]{:S(2)}) copy-start(f32[101]{0:T(128)} %param.39) | copy-start | bytes 1216
  205.9 70.8 %copy-start.15 = (bf16[256,101]{0,1:T(8,128)(2,1)S(1)}, bf16[256,101]{0,1:T(8,128)(2,1)}, u32[]{:S(2)}) copy-start(bf16[256,101]{0,1:T(8,128)(2,1)} %param.38) | copy-start | bytes 155140
  206.0 205.8 %all-reduce.14.cloned.1.call-start = ((), (), s32[]{:S(2)}) async-start(), calls=%async_computation.7 | async-start | bytes 262144 | tf_op jit(solution)/shard_map/psum | solution.py:118
  267.5 5.2 copy-start.3
  272.7 10.0 %slice-start.4 = ((s8[8388608]{0:T(1024)(128)(4,1)}), s8[4194304]{0:T(1024)(128)(4,1)S(1)}, s32[]{:S(2)}) async-start(s8[8388608]{0:T(1024)(128)(4,1)} %bitcast.221), calls=%async_computation.13 | async-start | bytes 8388608
  276.7 5.9 slice-start.5
  328.0 38.5 %slice-start = ((s8[16777216]{0:T(1024)(128)(4,1)}), s8[4194304]{0:T(1024)(128)(4,1)S(1)}, s32[]{:S(2)}) async-start(s8[16777216]{0:T(1024)(128)(4,1)} %bitcast.217), calls=%async_computation.9 | async-start | bytes 8388608
  337.2 29.3 %slice-start.1 = ((s8[16777216]{0:T(1024)(128)(4,1)}), s8[4194304]{0:T(1024)(128)(4,1)S(1)}, s32[]{:S(2)}) async-start(s8[16777216]{0:T(1024)(128)(4,1)} %bitcast.217), calls=%async_computation.10 | async-start | bytes 8388608
  337.2 29.3 %slice-start.2 = ((s8[16777216]{0:T(1024)(128)(4,1)}), s8[4194304]{0:T(1024)(128)(4,1)S(1)}, s32[]{:S(2)}) async-start(s8[16777216]{0:T(1024)(128)(4,1)} %bitcast.217), calls=%async_computation.11 | async-start | bytes 8388608
  337.2 29.3 %slice-start.3 = ((s8[16777216]{0:T(1024)(128)(4,1)}), s8[4194304]{0:T(1024)(128)(4,1)S(1)}, s32[]{:S(2)}) async-start(s8[16777216]{0:T(1024)(128)(4,1)} %bitcast.217), calls=%async_computation.12 | async-start | bytes 8388608
  375.2 174.5 %all-reduce.12.cloned.1.call-start = ((), (), s32[]{:S(2)}) async-start(), calls=%async_computation.6 | async-start | bytes 3784704 | tf_op jit(solution)/shard_map/psum | solution.py:141
  413.5 13.0 %copy-start.12 = (bf16[6,8192]{1,0:T(8,128)(2,1)S(1)}, bf16[6,8192]{1,0:T(8,128)(2,1)}, u32[]{:S(2)}) copy-start(bf16[6,8192]{1,0:T(8,128)(2,1)} %copy-done.11) | copy-start | bytes 294916
  426.5 3.2 copy-start.2
  426.5 3.2 copy-start.17
  432.3 9.8 %copy-start.9 = (f32[80,512]{1,0:T(8,128)}, f32[80,512]{1,0:T(8,128)S(1)}, u32[]{:S(2)}) copy-start(f32[80,512]{1,0:T(8,128)S(1)} %fusion.30) | copy-start | bytes 491524
  432.4 9.8 %copy-start.22 = (bf16[80,96]{1,0:T(8,128)(2,1)S(1)}, bf16[80,96]{1,0:T(8,128)(2,1)}, u32[]{:S(2)}) copy-start(bf16[80,96]{1,0:T(8,128)(2,1)} %param.27) | copy-start | bytes 46084
  432.4 11.3 %copy-start.8 = (bf16[614,512]{1,0:T(8,128)(2,1)S(1)}, bf16[614,512]{1,0:T(8,128)(2,1)}, u32[]{:S(2)}) copy-start(bf16[614,512]{1,0:T(8,128)(2,1)} %copy-done.7) | copy-start | bytes 1886212
  443.6 172.8 %reduce-scatter.9.cloned.1.call-start = ((), (), s32[]{:S(2)}) async-start(), calls=%async_computation.5 | async-start | bytes 10485760
  465.8 1.6 copy-start.5
  465.8 1.6 copy-start.25
  471.9 8.9 %copy-start.10 = (f32[80,512]{1,0:T(8,128)S(1)}, f32[80,512]{1,0:T(8,128)}, u32[]{:S(2)}) copy-start(f32[80,512]{1,0:T(8,128)} %copy-done.9) | copy-start | bytes 491524
  476.0 146.8 %copy-start.1 = (bf16[256,512]{1,0:T(8,128)(2,1)S(1)}, bf16[256,512]{1,0:T(8,128)(2,1)}, u32[]{:S(2)}) copy-start(bf16[256,512]{1,0:T(8,128)(2,1)} %param.36) | copy-start | bytes 786436
  549.7 71.7 %copy-start.13 = (f32[256,512]{1,0:T(8,128)S(1)}, f32[256,512]{1,0:T(8,128)}, u32[]{:S(2)}) copy-start(f32[256,512]{1,0:T(8,128)} %get-tuple-element.108) | copy-start | bytes 1572868
  549.7 72.5 %copy-start.20 = (f32[256,101]{0,1:T(8,128)S(1)}, f32[256,101]{0,1:T(8,128)}, u32[]{:S(2)}) copy-start(f32[256,101]{0,1:T(8,128)} %get-tuple-element.110) | copy-start | bytes 310276
Sparse Core Ops, SparseCore 0:
  49.7 34.1 all-reduce.15
  120.6 71.7 reduce-scatter.6
  194.8 72.6 all-reduce.9
  269.5 58.3 all-gather.1
  375.3 31.5 all-reduce.13
  443.7 98.5 all-reduce.11
  544.9 71.4 reduce-scatter.8
where the time goes:
time: 637 us; the launch traced here: 630 us
  waiting for transfers between devices  263 us (41%)
  other arithmetic  136 us (21%)
  matrix products  102 us (16%)
  blocking collectives  64.2 us (10%)
  local copies, waits for them, and re-layouts  47.8 us (8%)
  between operations  15.8 us (2%)
    unnamed x9, waiting for transfers between devices  126 us
    dot_general x9, matrix products, contract(): lax.dot_general(left, right, (((left_dim,), (right_dim,)), ((), ())), pre...  68 us
    psum x1, waiting for transfers between devices, on_device(): logits = lax.psum(logit_part, 'mp') + rew_b2  59.5 us
    all_gather x1, waiting for transfers between devices, on_device(): d_full = lax.all_gather(d_share, 'mp', axis=1, tiled=True)  43.2 us
    unnamed x86, local copies, waits for them, and re-layouts  41.7 us
    psum x1, blocking collectives, on_device(): lax.psum((cons_part, rew_part, embed_part), ('dp', 'mp'))  41.2 us
    psum x1, waiting for transfers between devices, on_device(): lax.psum((jnp.sum(pre_act, axis=2).T, jnp.sum(pre_act * pre_act, axis=2)....  34 us
    another operation x1, other arithmetic, on_device(): d_hidden = jnp.stack([d_hid_dyn, d_hid_rew], axis=1)  29.3 us
  transfers between devices with their start and end apart: 7, of which 5 were waited for; matrix products, arithmetic and copies ran while one was open for 19% of the time, Pallas kernels for 0%

commit v1 on v0

--- a/solution.py
+++ b/solution.py
@@ -2,6 +2,7 @@
 import jax.numpy as jnp
 from jax import lax
 from jax.sharding import PartitionSpec as P
+from jax.lax import axis_index, axis_size, ppermute
 
 HID = 1024
 GROUP = 8
@@ -100,7 +101,19 @@
     d_groups = (2.0 * CONS_COEF / total_rows * lat_error).reshape(groups.shape)
     d_lat = simplex * (d_groups - jnp.sum(simplex * d_groups, axis=-1, keepdims=True))
     d_share = d_lat.reshape(tok_rows, share_width).astype(jnp.bfloat16)
-    d_full = lax.all_gather(d_share, "mp", axis=1, tiled=True)
+    nd = axis_size("mp")
+    samples = tuple(((to_i, (to_i + 1) % nd) for to_i in range(nd)))
+    pool = tuple(((to_i, (to_i - 1) % nd) for to_i in range(nd)))
+    z1, outcome_arr = ([d_share], [d_share])
+    for _ in range(nd // 2):
+        z1.append(ppermute(z1[-1], "mp", samples))
+    for _ in range((nd - 1) // 2):
+        outcome_arr.append(ppermute(outcome_arr[-1], "mp", pool))
+    d_full = jnp.roll(
+        jnp.concatenate([*z1[::-1], *outcome_arr[1:]], axis=1),
+        shift=(axis_index("mp") - nd // 2) * d_share.shape[1],
+        axis=1,
+    )
     d_logits = (REW_COEF / total_rows * (jnp.exp(log_probs) - target)).astype(jnp.bfloat16)
     grad_w2_dyn = contract(hidden_dyn, d_full, 0, 0)
     grad_b2_dyn = jnp.sum(d_full.astype(jnp.float32), axis=0)

time: 637 us -> 680 us (1.068)
  local copies, waits for them, and re-layouts: 47.8 us -> 67.4 us
  waiting for transfers between devices: 263 us -> 279 us
  starting transfers between devices: 1.22 us -> 13.7 us
    ppermute x0 -> x3, waiting for transfers between devices: none -> 65.5 us  [the longest x2 49.7 us: on_device(): z1.append(ppermute(z1[-1], 'mp', samples))]
    all_gather x1 -> x0, waiting for transfers between devices: 43.2 us -> none  [on_device(): d_full = lax.all_gather(d_share, 'mp', axis=1, tiled=True)]
    unnamed x86 -> x95, local copies, waits for them, and re-layouts: 41.7 us -> 59.7 us
    ppermute x0 -> x3, starting transfers between devices: none -> 13.1 us  [the longest x2 13.1 us: on_device(): z1.append(ppermute(z1[-1], 'mp', samples))]
    psum x1, waiting for transfers between devices: 59.5 us -> 48.4 us  [on_device(): logits = lax.psum(logit_part, 'mp') + rew_b2]
    unnamed x9 -> x8, waiting for transfers between devices: 126 us -> 132 us
  transfers between devices with their start and end apart: 7 -> 9, of which waited for: 5 -> 6; matrix products, arithmetic and copies ran while one was open for 19% -> 17% of each run, Pallas kernels for 0% -> 0%
where the time goes in v1:
time: 680 us; the launch traced here: 673 us
  waiting for transfers between devices  279 us (41%)
  other arithmetic  134 us (20%)
  matrix products  97.5 us (14%)
  local copies, waits for them, and re-layouts  67.4 us (10%)
  blocking collectives  65.8 us (10%)
  between operations  15.6 us (2%)
  starting transfers between devices  13.7 us (2%)
    unnamed x8, waiting for transfers between devices  132 us
    dot_general x9, matrix products, contract(): lax.dot_general(left, right, (((left_dim,), (right_dim,)), ((), ())), pre...  66.6 us
    unnamed x95, local copies, waits for them, and re-layouts  59.7 us
    ppermute x2, waiting for transfers between devices, on_device(): z1.append(ppermute(z1[-1], 'mp', samples))  49.7 us
    psum x1, waiting for transfers between devices, on_device(): logits = lax.psum(logit_part, 'mp') + rew_b2  48.4 us
    psum x1, blocking collectives, on_device(): lax.psum((cons_part, rew_part, embed_part), ('dp', 'mp'))  43 us
    psum x1, waiting for transfers between devices, on_device(): lax.psum((jnp.sum(pre_act, axis=2).T, jnp.sum(pre_act * pre_act, axis=2)....  33.9 us
    reduce_sum x1, other arithmetic, on_device(): grad_shift = jnp.sum(d_normed, axis=0)  28.9 us
  transfers between devices with their start and end apart: 9, of which 6 were waited for; matrix products, arithmetic and copies ran while one was open for 17% of the time, Pallas kernels for 0%

profile of v1, /device:TPU:0, one launch (start us, length us, event | category | flops | bytes accessed | tf_op | source)
XLA Modules:
  0.0 673.3 jit_solution(2645775570115903853)
XLA Ops:
  7.2 1.0 constant_dynamic-update-slice_fusion.1
  9.0 1.0 constant_dynamic-update-slice_fusion
  10.0 11.8 %fusion.41 = f32[512,8192]{1,0:T(8,128)} fusion(bf16[8192,512]{1,0:T(8,128)(2,1)} %param.20, bf16[614,512]{1,0:T(8,128)(2,1)S(1)} %constant_dynamic-update-slice_fusion), kind=kOutput, calls=%fused_computation.97 | convolution fusion | flops 4294967296 | bytes 25690112 | tf_op jit(solution)/shard_map/dot_general | solution.py:65
  21.8 7.2 %fusion.35 = f32[8192,512]{0,1:T(8,128)} fusion(bf16[80,96]{1,0:T(8,128)(2,1)S(1)} %copy-done.19, s32[8192]{0:T(1024)S(1)} %copy-done.16, bf16[614,512]{1,0:T(8,128)(2,1)S(1)} %constant_dynamic-update-slice_fusion), kind=kOutput, calls=%fused_computation.89 | convolution fusion | flops 932577280 | bytes 16928768 | tf_op jit(solution)/shard_map/dot_general | solution.py:67
  29.6 19.9 %bitcast_reduce_fusion = (f32[8192,2]{0,1:T(2,128)}, f32[8192,2]{0,1:T(2,128)}, f32[8192,512]{0,1:T(8,128)}) fusion(f32[512]{0:T(512)S(1)} %pad_maximum_fusion.2, f32[8192,512]{0,1:T(8,128)} %fusion.35, bf16[6,8192]{1,0:T(8,128)(2,1)S(1)} %fusion.23, bf16[614,512]{1,0:T(8,128)(2,1)S(1)} %constant_dynamic-update-slice_fusion, f32[512,8192]{1,0:T(8,128)} %fusion.41), kind=kOutput, calls=%fused_computation.29 | convolution fusion | flops 75464704 | bytes 50604032 | tf_op jit(solution)/shard_map/dot_general | solution.py:18
  50.0 33.9 %all-reduce.16.cloned.1.call-done = (f32[2,8192]{1,0:T(2,128)}, f32[2,8192]{1,0:T(2,128)}) async-done(((f32[2,8192]{1,0:T(2,128)}, f32[2,8192]{1,0:T(2,128)}), (f32[2,8192]{1,0:T(2,128)}, f32[2,8192]{1,0:T(2,128)})) %all-reduce.16.cloned.1.call-update) | async-done | bytes 131088 | tf_op jit(solution)/shard_map/psum | solution.py:71
  83.8 0.9 multiply_bitcast_fusion.2
  84.8 14.7 %fusion.17 = bf16[8192,2,256]{0,2,1:T(8,128)(2,1)S(1)} fusion(f32[8192,512]{0,1:T(8,128)} %get-tuple-element.93, f32[2,256]{1,0:T(2,128)S(1)} %get-tuple-element.92, f32[2,256]{1,0:T(2,128)S(1)} %get-tuple-element.94, f32[8192,2]{0,1:T(2,128)S(1)} %get-tuple-element.82, f32[8192,2]{0,1:T(2,128)S(1)} %get-tuple-element.81), kind=kLoop, calls=%fused_computation.41 | loop fusion | flops 50331648 | bytes 25300992 | tf_op jit(solution)/shard_map/convert_element_type | solution.py:81
  99.5 3.2 copy-done.4
  102.8 5.6 convolution_convert_fusion.1
  108.4 11.4 %copy.47 = bf16[8192,512]{0,1:T(8,128)(2,1)} copy(bf16[8192,512]{1,0:T(8,128)(2,1)} %convolution_convert_fusion.1) | data formatting | bytes 16777216
  119.9 1.5 copy-done.6
  121.4 2.9 copy.45
  125.0 66.7 %reduce-scatter.7.cloned.1.call-done = bf16[128,8192]{1,0:T(8,128)(2,1)} async-done(((bf16[512,8192]{1,0:T(8,128)(2,1)}), bf16[128,8192]{1,0:T(8,128)(2,1)}) %reduce-scatter.7.cloned.1.call-update) | async-done | bytes 2097168
  191.7 3.0 bitcast_reduce_fusion.1
  194.8 3.5 fusion.29
  198.3 7.5 %fusion.21 = bf16[8192,128]{0,1:T(8,128)(2,1)S(1)} fusion(bf16[8192,128]{0,1:T(8,128)(2,1)} %copy.45, bf16[128,8192]{1,0:T(8,128)(2,1)} %reduce-scatter.7.cloned.1.call-done, f32[8192,16]{0,1:T(8,128)S(1)} %fusion.29, f32[8192,16]{0,1:T(8,128)S(1)} %bitcast_reduce_fusion.1, f32[128]{0:T(128)} %copy-done.22), kind=kOutput, calls=%fused_computation.52 | output fusion | flops 21102600 | bytes 7340544 | tf_op jit(solution)/shard_map/sub | solution.py:102
  205.8 13.1 %collective-permute-start = (bf16[8192,128]{0,1:T(8,128)(2,1)S(1)}, bf16[8192,128]{0,1:T(8,128)(2,1)}, u32[]{:S(2)}, u32[]{:S(2)}) collective-permute-start(bf16[8192,128]{0,1:T(8,128)(2,1)S(1)} %fusion.21), channel_id=1, source_target_pairs={{0,1},{1,2},{2,3},{3,0},{4,5},{5,6},{6,7},{7,4},{8,9},{9,10},{10,1... | collective-permute-start | bytes 6291464 | tf_op jit(solution)/shard_map/ppermute | solution.py:109
  218.9 2.5 fusion.31
  222.1 49.7 %collective-permute-done = bf16[8192,128]{0,1:T(8,128)(2,1)} collective-permute-done((bf16[8192,128]{0,1:T(8,128)(2,1)S(1)}, bf16[8192,128]{0,1:T(8,128)(2,1)}, u32[]{:S(2)}, u32[]{:S(2)}) %collective-permute-start) | collective-permute-done | bytes 2097184 | tf_op jit(solution)/shard_map/ppermute | solution.py:109
  271.8 1.4 broadcast_add_fusion
  273.2 1.4 broadcast_subtract_fusion
  274.5 48.4 %all-reduce.10.cloned.1.call-done = f32[8192,101]{0,1:T(8,128)} async-done(((f32[8192,101]{0,1:T(8,128)}), f32[8192,101]{0,1:T(8,128)}) %all-reduce.10.cloned.1.call-update) | async-done | bytes 3309584 | tf_op jit(solution)/shard_map/psum | solution.py:90
  323.0 2.5 add_reduce_fusion
  325.5 2.6 exponential_reduce_fusion
  328.2 3.5 convert_reduce_fusion.2
  331.7 4.6 convolution_bitcast_fusion.1
  336.3 2.1 fusion.30
  338.4 3.1 constant_dynamic-update-slice_fusion.9
  341.5 3.2 constant_dynamic-update-slice_fusion.8
  344.7 1.5 constant_dynamic-update-slice_fusion.7
  346.1 15.8 %collective-permute-done.2 = bf16[8192,128]{0,1:T(8,128)(2,1)S(1)} collective-permute-done((bf16[8192,128]{0,1:T(8,128)(2,1)S(1)}, bf16[8192,128]{0,1:T(8,128)(2,1)S(1)}, u32[]{:S(2)}, u32[]{:S(2)}) %collective-permute-start.2) | collective-permute-done | bytes 2097184 | tf_op jit(solution)/shard_map/ppermute | solution.py:111
  362.0 1.5 constant_dynamic-update-slice_fusion.6
  363.5 3.3 constant_dynamic-update-slice_fusion.5
  366.8 3.1 constant_dynamic-update-slice_fusion.4
  369.9 1.5 constant_dynamic-update-slice_fusion.3
  371.4 1.5 constant_dynamic-update-slice_fusion.2
  372.9 9.1 %convolution_bitcast_fusion = f32[8192,1,256]{0,2,1:T(8,128)} fusion(bf16[256,512]{1,0:T(8,128)(2,1)S(1)} %copy-done, bf16[8192,1024]{0,1:T(8,128)(2,1)} %constant_dynamic-update-slice_fusion.2, s32[]{:T(128)S(6)} %select_n.55), kind=kOutput, calls=%fused_computation.47 | convolution fusion | flops 2147483648 | bytes 17039364 | tf_op jit(solution)/shard_map/dot_general | solution.py:18
  382.0 25.9 %pad_maximum_fusion = (f32[8192,2,256]{0,2,1:T(8,128)}, f32[8192,2,256]{0,2,1:T(8,128)}) fusion(f32[8192,1,256]{0,2,1:T(8,128)} %convolution_bitcast_fusion.1, f32[8192,1,256]{0,2,1:T(8,128)} %convolution_bitcast_fusion, f32[2,256]{1,0:T(2,128)S(1)} %get-tuple-element.92, f32[2,256]{1,0:T(2,128)S(1)} %get-tuple-element.94, ...), kind=kLoop, calls=%fused_computation.19 | loop fusion | flops 104857600 | bytes 67244032 | tf_op jit(solution)/shard_map/stack | solution.py:125
  407.9 8.7 %fusion.55 = (f32[8192,2]{0,1:T(2,128)}, f32[8192,2]{0,1:T(2,128)}) fusion(f32[8192,2,256]{0,2,1:T(8,128)} %get-tuple-element.75, f32[8192,2]{0,1:T(2,128)S(1)} %get-tuple-element.82, f32[8192,2]{0,1:T(2,128)S(1)} %get-tuple-element.81, f32[8192,512]{0,1:T(8,128)S(1)} %bitcast.216), kind=kLoop, calls=%fused_computation.131 | loop fusion | flops 20938752 | bytes 33816576 | tf_op jit(solution)/shard_map/reduce_sum | solution.py:132
  416.7 7.8 %fusion.24 = f32[256,512]{1,0:T(8,128)} fusion(bf16[8192,1024]{0,1:T(8,128)(2,1)} %constant_dynamic-update-slice_fusion.2, s32[]{:T(128)S(6)} %select_n.55, bf16[8192,2,256]{0,2,1:T(8,128)(2,1)} %copy-done.4), kind=kOutput, calls=%fused_computation.57 | convolution fusion | flops 2147483648 | bytes 13107204 | tf_op jit(solution)/shard_map/dot_general | solution.py:18
  424.5 28.9 %fusion.54 = (f32[512]{0:T(512)S(1)}, f32[512]{0:T(512)S(1)}, f32[8192,512]{0,1:T(8,128)}) fusion(f32[8192,2]{0,1:T(2,128)S(1)} %get-tuple-element.82, f32[8192,512]{0,1:T(8,128)} %get-tuple-element.93, f32[8192,2]{0,1:T(2,128)S(1)} %get-tuple-element.81, f32[512]{0:T(512)S(1)} %bitcast.230, f32[512]{0:T(512)S(1)} %bitcast.228, ...), kind=kLoop, calls=%fused_computation.130 | loop fusion | flops 109050880 | bytes 50470912 | tf_op jit(solution)/shard_map/reduce_sum | solution.py:129
  453.4 0.9 multiply_bitcast_fusion
  454.3 0.9 multiply_bitcast_fusion.1
  455.2 12.9 %convert_reduce_fusion.1 = (f32[512]{0:T(512)S(1)}, bf16[8192,512]{0,1:T(8,128)(2,1)S(1)}) fusion(f32[8192,2]{0,1:T(2,128)S(1)} %multiply_bitcast_fusion, f32[8192,512]{0,1:T(8,128)} %get-tuple-element.93, f32[8192,2]{0,1:T(2,128)S(1)} %get-tuple-element.81, f32[8192,2]{0,1:T(2,128)S(1)} %multiply_bitcast_fusion.1, f32[8192,512]{0,1:T(8,128)} %get-tuple-element.71, ...), kind=kLoop, calls=%fused_computation.37 | loop fusion | flops 41942528 | bytes 42209280 | tf_op jit(solution)/shard_map/reduce_sum | solution.py:138
  468.1 2.3 fusion.62
  470.4 0.9 copy-done.2
  471.3 2.7 fusion.32
  474.0 9.7 %convolution_bitcast_fusion.3 = f32[512,512]{1,0:T(8,128)S(1)} fusion(bf16[8192,512]{0,1:T(8,128)(2,1)} %copy-done.2, bf16[8192,512]{1,0:T(8,128)(2,1)} %param.20), kind=kOutput, calls=%fused_computation.90 | convolution fusion | flops 4294967296 | bytes 17825792 | tf_op jit(solution)/shard_map/dot_general | solution.py:18
  484.0 1.2 pad_maximum_fusion.1
  485.3 10.3 %convolution_convert_fusion = bf16[8192,512]{1,0:T(8,128)(2,1)} fusion(bf16[8192,512]{0,1:T(8,128)(2,1)} %copy-done.2, bf16[614,512]{1,0:T(8,128)(2,1)S(1)} %copy-done.8), kind=kOutput, calls=%fused_computation.45 | convolution fusion | flops 4299161600 | bytes 17301504 | tf_op jit(solution)/shard_map/dot_general | solution.py:18
  495.6 11.3 %copy.49 = bf16[8192,512]{0,1:T(8,128)(2,1)} copy(bf16[8192,512]{1,0:T(8,128)(2,1)} %convolution_convert_fusion) | data formatting | bytes 16777216
  507.7 0.8 copy-done.5
  508.5 4.5 multiply_reduce_fusion.2
  513.0 4.1 copy.46
  517.2 4.6 convert_reduce_fusion
  521.8 1.1 fusion.43
  522.9 43.0 %all-reduce = (f32[1]{0:T(128)}, f32[1]{0:T(128)}, f32[80,96]{1,0:T(8,128)}) all-reduce(f32[1]{0:T(128)} %bitcast.30, f32[1]{0:T(128)} %bitcast.29, f32[80,96]{1,0:T(8,128)S(1)} %fusion.43), channel_id=1, replica_groups=mesh['dp'=8,'mp'=4] {'dp','mp'}, use_global_device_ids=true, to_apply=%region_19.20 | all-reduce | flops 7682 | bytes 61456 | tf_op jit(solution)/shard_map/psum | solution.py:152
  565.9 22.8 %all-reduce.1 = (f32[512]{0:T(512)S(1)}, f32[2,256]{1,0:T(2,128)S(1)}, f32[2,256]{1,0:T(2,128)S(1)}, f32[512]{0:T(512)}, f32[101]{0:T(128)}) all-reduce(f32[512]{0:T(512)S(1)} %get-tuple-element.72, f32[2,256]{1,0:T(2,128)S(1)} %reduce_sum.142, f32[2,256]{1,0:T(2,128)S(1)} %reduce_sum.144, ...), channel_id=1, replica_groups=mesh['dp'=8,'mp'=4] {'dp'}, use_global_device_ids=true, to_apply=%region_23.24 | all-reduce | flops 2149 | bytes 17192 | tf_op jit(solution)/shard_map/psum | solution.py:154
  588.7 1.9 maximum_multiply_fusion
  592.3 2.7 fusion.58
  595.0 64.9 %reduce-scatter.9.cloned.1.call-done = bf16[128,8192]{1,0:T(8,128)(2,1)} async-done(((bf16[512,8192]{1,0:T(8,128)(2,1)}), bf16[128,8192]{1,0:T(8,128)(2,1)}) %reduce-scatter.9.cloned.1.call-update) | async-done | bytes 2097168
  659.9 3.2 copy.50
  663.1 1.7 multiply_convert_fusion
  (109 shorter events, 7.0 us)
Async XLA Ops:
  7.2 95.6 %copy-start = (bf16[256,512]{1,0:T(8,128)(2,1)S(1)}, bf16[256,512]{1,0:T(8,128)(2,1)}, u32[]{:S(2)}) copy-start(bf16[256,512]{1,0:T(8,128)(2,1)} %param.36) | copy-start | bytes 786436
  7.2 76.6 %all-reduce.16.cloned.1.call-start = ((), (), s32[]{:S(2)}) async-start(), calls=%async_computation.7 | async-start | bytes 262144 | tf_op jit(solution)/shard_map/psum | solution.py:71
  10.0 19.6 %copy-start.7 = (bf16[614,512]{1,0:T(8,128)(2,1)}, bf16[614,512]{1,0:T(8,128)(2,1)S(1)}, u32[]{:S(2)}) copy-start(bf16[614,512]{1,0:T(8,128)(2,1)S(1)} %constant_dynamic-update-slice_fusion) | copy-start | bytes 1886212
  10.0 11.8 %copy-start.16 = (s32[8192]{0:T(1024)S(1)}, s32[8192]{0:T(1024)}, u32[]{:S(2)}) copy-start(s32[8192]{0:T(1024)} %param.22) | copy-start | bytes 98308
  10.0 11.8 %copy-start.19 = (bf16[80,96]{1,0:T(8,128)(2,1)S(1)}, bf16[80,96]{1,0:T(8,128)(2,1)}, u32[]{:S(2)}) copy-start(bf16[80,96]{1,0:T(8,128)(2,1)} %param.27) | copy-start | bytes 46084
  21.8 7.2 %copy-start.29 = (bf16[6,8192]{1,0:T(8,128)(2,1)S(1)}, bf16[6,8192]{1,0:T(8,128)(2,1)}, u32[]{:S(2)}) copy-start(bf16[6,8192]{1,0:T(8,128)(2,1)} %param.21) | copy-start | bytes 294916
  21.8 7.2 %copy-start.30 = (s32[80,6]{0,1:T(8,128)S(1)}, s32[80,6]{0,1:T(8,128)}, u32[]{:S(2)}) copy-start(s32[80,6]{0,1:T(8,128)} %param.23) | copy-start | bytes 5764
  29.5 19.9 %copy-start.11 = (bf16[6,8192]{1,0:T(8,128)(2,1)}, bf16[6,8192]{1,0:T(8,128)(2,1)S(1)}, u32[]{:S(2)}) copy-start(bf16[6,8192]{1,0:T(8,128)(2,1)S(1)} %fusion.23) | copy-start | bytes 294916
  29.6 20.4 %copy-start.25 = (f32[256]{0:T(256)S(1)}, f32[256]{0:T(256)}, u32[]{:S(2)}) copy-start(f32[256]{0:T(256)} %param.35) | copy-start | bytes 3076
  29.6 20.4 %copy-start.26 = (f32[256]{0:T(256)S(1)}, f32[256]{0:T(256)}, u32[]{:S(2)}) copy-start(f32[256]{0:T(256)} %param.31) | copy-start | bytes 3076
  29.6 20.4 %copy-start.27 = (f32[256]{0:T(256)S(1)}, f32[256]{0:T(256)}, u32[]{:S(2)}) copy-start(f32[256]{0:T(256)} %param.34) | copy-start | bytes 3076
  29.6 20.4 %copy-start.28 = (f32[256]{0:T(256)S(1)}, f32[256]{0:T(256)}, u32[]{:S(2)}) copy-start(f32[256]{0:T(256)} %param.30) | copy-start | bytes 3076
  49.5 142.2 %reduce-scatter.7.cloned.1.call-start = ((), (), s32[]{:S(2)}) async-start(), calls=%async_computation.3 | async-start | bytes 10485760
  99.5 3.2 copy-start.4
  119.8 1.6 copy-start.6
  119.8 203.1 %all-reduce.10.cloned.1.call-start = ((), (), s32[]{:S(2)}) async-start(), calls=%async_computation.2 | async-start | bytes 6815744 | tf_op jit(solution)/shard_map/psum | solution.py:90
  125.0 69.7 %copy-start.22 = (f32[128]{0:T(128)}, f32[128]{0:T(128)S(1)}, u32[]{:S(2)}) copy-start(f32[128]{0:T(128)S(1)} %dynamic_slice.7) | copy-start | bytes 1540
  194.8 24.1 %slice-start.4 = ((s8[8388608]{0:T(1024)(128)(4,1)}), s8[4194304]{0:T(1024)(128)(4,1)S(1)}, s32[]{:S(2)}) async-start(s8[8388608]{0:T(1024)(128)(4,1)} %bitcast.219), calls=%async_computation.12 | async-start | bytes 8388608
  198.3 20.6 %slice-start.5 = ((s8[8388608]{0:T(1024)(128)(4,1)}), s8[4194304]{0:T(1024)(128)(4,1)S(1)}, s32[]{:S(2)}) async-start(s8[8388608]{0:T(1024)(128)(4,1)} %bitcast.219), calls=%async_computation.13 | async-start | bytes 8388608
  198.3 20.6 %copy-start.14 = (bf16[256,101]{0,1:T(8,128)(2,1)S(1)}, bf16[256,101]{0,1:T(8,128)(2,1)}, u32[]{:S(2)}) copy-start(bf16[256,101]{0,1:T(8,128)(2,1)} %param.38) | copy-start | bytes 155140
  205.8 66.0 %collective-permute-start = (bf16[8192,128]{0,1:T(8,128)(2,1)S(1)}, bf16[8192,128]{0,1:T(8,128)(2,1)}, u32[]{:S(2)}, u32[]{:S(2)}) collective-permute-start(bf16[8192,128]{0,1:T(8,128)(2,1)S(1)} %fusion.21), channel_id=1, source_target_pairs={{0,1},{1,2},{2,3},{3,0},{4,5},{5,6},{6,7},{7,4},{8,9},{9,10},{10,1... | collective-permute-start | bytes 6291464 | tf_op jit(solution)/shard_map/ppermute | solution.py:109
  221.4 232.0 %all-reduce.14.cloned.1.call-start = ((), (), s32[]{:S(2)}) async-start(), calls=%async_computation.6 | async-start | bytes 262144 | tf_op jit(solution)/shard_map/psum | solution.py:131
  271.8 66.7 %collective-permute-start.1 = (bf16[8192,128]{0,1:T(8,128)(2,1)}, bf16[8192,128]{0,1:T(8,128)(2,1)}, u32[]{:S(2)}, u32[]{:S(2)}) collective-permute-start(bf16[8192,128]{0,1:T(8,128)(2,1)} %collective-permute-done), channel_id=1, source_target_pairs={{0,1},{1,2},{2,3},{3,0},{4,5},{5,6},{6,7},{7,4},{8,9},{9,10},{10,1... | collective-permute-start | bytes 6291464 | tf_op jit(solution)/shard_map/ppermute | solution.py:109
  323.0 5.2 copy-start.3
  323.0 8.7 %copy-start.15 = (bf16[256,101]{0,1:T(8,128)(2,1)S(1)}, bf16[256,101]{0,1:T(8,128)(2,1)}, u32[]{:S(2)}) copy-start(bf16[256,101]{0,1:T(8,128)(2,1)} %param.38) | copy-start | bytes 155140
  328.1 8.2 %slice-start.6 = ((s8[8388608]{0:T(1024)(128)(4,1)}), s8[4194304]{0:T(1024)(128)(4,1)S(1)}, s32[]{:S(2)}) async-start(s8[8388608]{0:T(1024)(128)(4,1)} %bitcast.221), calls=%async_computation.14 | async-start | bytes 8388608
  331.7 4.6 slice-start.7
  338.4 23.6 %collective-permute-start.2 = (bf16[8192,128]{0,1:T(8,128)(2,1)S(1)}, bf16[8192,128]{0,1:T(8,128)(2,1)S(1)}, u32[]{:S(2)}, u32[]{:S(2)}) collective-permute-start(bf16[8192,128]{0,1:T(8,128)(2,1)S(1)} %fusion.21), channel_id=1, source_target_pairs={{0,3},{1,0},{2,1},{3,2},{4,7},{5,4},{6,5},{7,6},{8,11},{9,8},{10,9... | collective-permute-start | bytes 6291464 | tf_op jit(solution)/shard_map/ppermute | solution.py:111
  363.5 18.5 %slice-start = ((s8[16777216]{0:T(1024)(128)(4,1)}), s8[4194304]{0:T(1024)(128)(4,1)S(1)}, s32[]{:S(2)}) async-start(s8[16777216]{0:T(1024)(128)(4,1)} %bitcast.215), calls=%async_computation.8 | async-start | bytes 8388608
  369.9 12.1 %slice-start.1 = ((s8[16777216]{0:T(1024)(128)(4,1)}), s8[4194304]{0:T(1024)(128)(4,1)S(1)}, s32[]{:S(2)}) async-start(s8[16777216]{0:T(1024)(128)(4,1)} %bitcast.215), calls=%async_computation.9 | async-start | bytes 8388608
  372.9 9.1 %slice-start.2 = ((s8[16777216]{0:T(1024)(128)(4,1)}), s8[4194304]{0:T(1024)(128)(4,1)S(1)}, s32[]{:S(2)}) async-start(s8[16777216]{0:T(1024)(128)(4,1)} %bitcast.215), calls=%async_computation.10 | async-start | bytes 8388608
  372.9 9.1 %slice-start.3 = ((s8[16777216]{0:T(1024)(128)(4,1)}), s8[4194304]{0:T(1024)(128)(4,1)S(1)}, s32[]{:S(2)}) async-start(s8[16777216]{0:T(1024)(128)(4,1)} %bitcast.215), calls=%async_computation.11 | async-start | bytes 8388608
  416.7 7.9 %copy-start.21 = (f32[1,2,2,128]{3,1,2,0:T(2,128)S(1)}, f32[1,2,2,128]{3,1,2,0:T(2,128)}, u32[]{:S(2)}) copy-start(f32[1,2,2,128]{3,1,2,0:T(2,128)} %copy.52) | copy-start | bytes 6148
  416.7 175.7 %all-reduce.12.cloned.1.call-start = ((), (), s32[]{:S(2)}) async-start(), calls=%async_computation.5 | async-start | bytes 3784704 | tf_op jit(solution)/shard_map/psum | solution.py:154
  455.2 13.0 %copy-start.12 = (bf16[6,8192]{1,0:T(8,128)(2,1)S(1)}, bf16[6,8192]{1,0:T(8,128)(2,1)}, u32[]{:S(2)}) copy-start(bf16[6,8192]{1,0:T(8,128)(2,1)} %copy-done.11) | copy-start | bytes 294916
  468.1 3.2 copy-start.2
  468.1 3.2 copy-start.17
  474.0 9.7 %copy-start.9 = (f32[80,512]{1,0:T(8,128)}, f32[80,512]{1,0:T(8,128)S(1)}, u32[]{:S(2)}) copy-start(f32[80,512]{1,0:T(8,128)S(1)} %fusion.32) | copy-start | bytes 491524
  474.0 9.7 %copy-start.20 = (bf16[80,96]{1,0:T(8,128)(2,1)S(1)}, bf16[80,96]{1,0:T(8,128)(2,1)}, u32[]{:S(2)}) copy-start(bf16[80,96]{1,0:T(8,128)(2,1)} %param.27) | copy-start | bytes 46084
  474.0 11.2 %copy-start.8 = (bf16[614,512]{1,0:T(8,128)(2,1)S(1)}, bf16[614,512]{1,0:T(8,128)(2,1)}, u32[]{:S(2)}) copy-start(bf16[614,512]{1,0:T(8,128)(2,1)} %copy-done.7) | copy-start | bytes 1886212
  485.2 174.7 %reduce-scatter.9.cloned.1.call-start = ((), (), s32[]{:S(2)}) async-start(), calls=%async_computation.4 | async-start | bytes 10485760
  506.9 1.6 copy-start.5
  506.9 1.6 copy-start.23
  508.5 57.4 %copy-start.24 = (f32[101]{0:T(128)S(1)}, f32[101]{0:T(128)}, u32[]{:S(2)}) copy-start(f32[101]{0:T(128)} %get-tuple-element.69) | copy-start | bytes 1216
  513.0 8.8 %copy-start.10 = (f32[80,512]{1,0:T(8,128)S(1)}, f32[80,512]{1,0:T(8,128)}, u32[]{:S(2)}) copy-start(f32[80,512]{1,0:T(8,128)} %copy-done.9) | copy-start | bytes 491524
  517.2 149.1 %copy-start.1 = (bf16[256,512]{1,0:T(8,128)(2,1)S(1)}, bf16[256,512]{1,0:T(8,128)(2,1)}, u32[]{:S(2)}) copy-start(bf16[256,512]{1,0:T(8,128)(2,1)} %param.36) | copy-start | bytes 786436
  592.3 72.5 %copy-start.13 = (f32[256,512]{1,0:T(8,128)S(1)}, f32[256,512]{1,0:T(8,128)}, u32[]{:S(2)}) copy-start(f32[256,512]{1,0:T(8,128)} %get-tuple-element.108) | copy-start | bytes 1572868
  592.3 73.3 %copy-start.18 = (f32[256,101]{0,1:T(8,128)S(1)}, f32[256,101]{0,1:T(8,128)}, u32[]{:S(2)}) copy-start(f32[256,101]{0,1:T(8,128)} %get-tuple-element.110) | copy-start | bytes 310276
Sparse Core Ops, SparseCore 0:
  49.6 34.1 all-reduce.15
  120.0 71.7 reduce-scatter.6
  221.6 101.3 all-reduce.9
  416.8 33.1 all-reduce.13
  485.3 100.8 all-reduce.11
  588.7 71.1 reduce-scatter.8
